TPU v7x, 256 devices: a whole 4x4x8 slice. The times are simulated.
256 devices in a mesh: grp: 8 (over y, core), sub: 32 (over z, x).
Axes of the slice: x: 4, y: 4, z: 8, core: 2. Of those that a mesh axis runs over, the one named last changes fastest.
Arguments:
- schur_block: float32 [8, 32, 1152, 1152], P('grp', 'sub')
- dirichlet_inverse: float32 [8, 32, 1152, 1152], P('grp', 'sub')
- coarse_basis: float32 [8, 32, 24, 1152], P('grp', 'sub'), may hold values from -0.3125 to 0.3125
- coarse_inverse: float32 [8, 768, 768], P('grp', None, 'sub')
- coarse_owner: int32 [8, 768], P('grp', 'sub'), may hold values from 0 to 767, each once within a row
- face_count: int32 [8, 32, 4], P('grp', 'sub'), may hold values from 0 to 384, as said below
- face_rows: int32 [8, 32, 4, 384], P('grp', 'sub'), may hold values from 0 to 1151, as said below
- multiplicity: int32 [8, 32, 1152], P('grp', 'sub'), may hold values from 1 to 5, as said below
- gradient: float32 [8, 32, 192, 1152], P('grp', 'sub'), may hold values from -6 to 6
- warm_start: float32 [8, 32, 192, 1152], P('grp', 'sub'), may hold values from -3 to 3
Outputs:
- adjoint: float32 [8, 32, 192, 1152], P('grp', 'sub')
Inputs may be any that keep to these rules, and one draw needn't show every extreme that they name: `coarse_owner`: each group's row names each coarse unknown once. `face_count`: faces across one grp or sub step have equal counts on both sides; faces 2 and 3 at the ends of sub have count 0; some face has count 384 in every draw. `face_rows`: the live entries of one face are distinct rows; entry k of a face and entry k of the matching face of the neighbour name the same unknown; a row may lie on several faces. `multiplicity`: one plus the number of live face entries that name the row.
All inputs are finite; a program needn't handle non-finite values.
Results may differ from a plain program's by a relative error of at most 0.00023.
Values sent between devices are 32-bit elements; how exact they have to be, the bound alone decides.
A program may use at most 128 MiB of HBM per device.

v0:
```python
import jax
import jax.numpy as jnp
from jax import lax
from jax.sharding import PartitionSpec as P

ITERS = 3
HIGHEST = lax.Precision.HIGHEST


def shifted(array, axis, by):
    peers = lax.axis_size(axis)
    return lax.ppermute(array, axis, [(i, (i + by) % peers) for i in range(peers)])


def from_behind(value, axis, steps):
    count = lax.axis_size(axis)
    first, last = (max(0, -steps), min(count, count - steps))
    return lax.ppermute(value, axis, [(source, source + steps) for source in range(first, last)])


def product(left, right):
    return jnp.dot(left, right, precision=HIGHEST, preferred_element_type=jnp.float32)


def local(
    schur_block,
    dirichlet_inverse,
    coarse_basis,
    coarse_inverse,
    coarse_owner,
    face_count,
    face_rows,
    multiplicity,
    gradient,
    warm_start,
):
    schur_local = schur_block[0, 0]
    dirichlet_local = dirichlet_inverse[0, 0]
    coarse_rows = coarse_basis[0, 0]
    face_index = face_rows[0, 0]
    live_mask = (jnp.arange(face_index.shape[1])[None, :] < face_count[0, 0][:, None]).astype(
        jnp.float32
    )
    weight = (1.0 / multiplicity[0, 0].astype(jnp.float32))[None, :]
    my_owner = coarse_owner[0]
    all_owner = lax.all_gather(coarse_owner, "sub", axis=1, tiled=True)[0]

    def assemble(values):
        outgoing = jax.vmap(lambda one_index, one_mask: values[:, one_index] * one_mask[None, :])(
            face_index, live_mask
        )
        from_next = shifted(outgoing[1], "grp", -1)
        from_prev = shifted(outgoing[0], "grp", 1)
        from_after = from_behind(outgoing[3], "sub", -1)
        from_before = from_behind(outgoing[2], "sub", 1)
        values = values.at[:, face_index[0]].add(from_next)
        values = values.at[:, face_index[1]].add(from_prev)
        values = values.at[:, face_index[2]].add(from_after)
        return values.at[:, face_index[3]].add(from_before)

    adjoint = warm_start[0, 0]
    right_side = gradient[0, 0]
    for iteration in range(ITERS):
        applied = product(adjoint, schur_local)
        residual = right_side - assemble(applied)
        weighted = residual * weight
        local_part = product(weighted, dirichlet_local)
        coarse_piece = lax.dot_general(
            weighted,
            coarse_rows,
            (((1,), (1,)), ((), ())),
            precision=HIGHEST,
            preferred_element_type=jnp.float32,
        )
        pieces = lax.all_gather(coarse_piece, "sub", axis=1, tiled=True)
        coarse_sum = jnp.zeros_like(pieces).at[:, all_owner].set(pieces)
        owned = product(coarse_sum, coarse_inverse[0])
        gathered = lax.all_gather(owned, "sub", axis=1, tiled=True)
        picked = gathered[:, my_owner]
        correction = product(picked, coarse_rows)
        adjoint = adjoint + assemble((local_part + correction) * weight)
    return adjoint[None, None]


def solution(mesh):
    in_specs = (
        P("grp", "sub", None, None),
        P("grp", "sub", None, None),
        P("grp", "sub", None, None),
        P("grp", None, "sub"),
        P("grp", "sub"),
        P("grp", "sub", None),
        P("grp", "sub", None, None),
        P("grp", "sub", None),
        P("grp", "sub", None, None),
        P("grp", "sub", None, None),
    )
    out_specs = P("grp", "sub", None, None)
    return jax.shard_map(local, mesh=mesh, in_specs=in_specs, out_specs=out_specs, check_vma=False)
```

profile of v0, /device:TPU:1, one launch (start us, length us, event | category | flops | bytes accessed | tf_op | source)
XLA Modules:
  0.0 631.9 jit_solution(7648857142585618406)
XLA Ops:
  1.5 11.3 %fusion.10 = f32[192,1152]{0,1:T(8,128)S(1)} fusion(f32[1,1,1152,1152]{3,2,1,0:T(8,128)} %param.10, f32[1,1,192,1152]{3,2,1,0:T(8,128)} %param.19), kind=kOutput, calls=%fused_computation.46 | convolution fusion | flops 3057647616 | bytes 7077888 | tf_op jit(solution)/shard_map/dot_general | solution.py:22
  12.8 4.7 gather_fusion
  17.5 1.7 multiply_bitcast_fusion.5
  19.3 4.0 collective-permute-start.3
  24.6 2.1 collective-permute-start.1
  28.1 22.5 %all-reduce = s32[768]{0:T(1024)S(1)} all-reduce(s32[768]{0:T(1024)S(1)} %bitcast_dynamic-update-slice_fusion), channel_id=1, replica_groups=mesh['grp'=8,'sub'=32] {'sub'}, use_global_device_ids=true, to_apply=%add | all-reduce | flops 768 | bytes 6144
  50.7 3.6 scatter_custom_fusion
  54.3 3.7 scatter_custom_fusion.1
  58.1 3.6 scatter_custom_fusion.2
  61.7 3.1 scatter_custom_fusion.3
  66.9 36.0 %all_gather.22 = f32[192,768]{0,1:T(8,128)S(1)} all-gather(f32[192,24]{0,1:T(8,128)S(1)} %fusion.97), channel_id=1, replica_groups=mesh['grp'=8,'sub'=32] {'sub'}, dimensions={1}, use_global_device_ids=true | all-gather | bytes 608256 | tf_op jit(solution)/shard_map/all_gather | solution.py:75
  102.9 6.3 scatter_custom_fusion.4
  110.9 41.2 %all_gather.23 = f32[192,768]{0,1:T(8,128)} all-gather(f32[192,24]{0,1:T(8,128)S(1)} %fusion.113), channel_id=1, replica_groups=mesh['grp'=8,'sub'=32] {'sub'}, dimensions={1}, use_global_device_ids=true | all-gather | bytes 608256 | tf_op jit(solution)/shard_map/all_gather | solution.py:78
  152.0 1.7 gather_fusion.1
  154.7 8.0 %bitcast_add_fusion = (f32[192,1152]{1,0:T(8,128)}, f32[192,1152]{1,0:T(8,128)}) fusion(f32[1,1,192,1152]{3,2,1,0:T(8,128)S(1)} %copy-done.6, f32[1152]{0:T(1024)S(1)} %divide_reduce_fusion, f32[192,1152]{1,0:T(8,128)S(1)} %fusion.106, f32[1,1,1152,1152]{3,2,1,0:T(8,128)} %param.11, f32[192,1152]{1,0:T(8,128)S(1)} %copy.31, ...), kind=kOutput, calls=%fused_computation.66 | convolution fusion | flops 3058753536 | bytes 10621440 | tf_op jit(solution)/shard_map/dot_general | solution.py:22
  164.2 4.7 gather_fusion.2
  171.8 28.8 %collective-permute-start.4 = (f32[192,384]{0,1:T(8,128)}, f32[192,384]{0,1:T(8,128)}, u32[]{:S(2)}, u32[]{:S(2)}) collective-permute-start(f32[192,384]{0,1:T(8,128)} %get-tuple-element.28), channel_id=1, source_target_pairs={{0,224},{32,0},{64,32},{96,64},{128,96},{160,128},{192,160},{224,1... | collective-permute-start | bytes 884744 | tf_op jit(solution)/shard_map/ppermute | solution.py:12
  203.0 4.7 collective-permute-start.7
  208.1 3.6 scatter_custom_fusion.5
  211.7 3.6 scatter_custom_fusion.6
  215.3 3.6 scatter_custom_fusion.7
  218.9 4.0 scatter_custom_fusion.8
  222.9 11.1 %fusion.8 = f32[192,1152]{0,1:T(8,128)S(1)} fusion(f32[192,1152]{0,1:T(8,128)S(1)} %scatter_custom_fusion.8, f32[1,1,1152,1152]{3,2,1,0:T(8,128)} %param.10), kind=kOutput, calls=%fused_computation.44 | convolution fusion | flops 3057647616 | bytes 7077888 | tf_op jit(solution)/shard_map/dot_general | solution.py:22
  234.0 4.7 gather_fusion.3
  241.4 1.7 collective-permute-start.9
  244.4 4.8 collective-permute-start.11
  249.2 3.6 scatter_custom_fusion.9
  252.8 3.7 scatter_custom_fusion.10
  256.5 3.6 scatter_custom_fusion.11
  260.1 3.6 scatter_custom_fusion.12
  264.9 2.1 fusion.94
  267.1 39.6 %all_gather.24 = f32[192,768]{0,1:T(8,128)S(1)} all-gather(f32[192,24]{0,1:T(8,128)S(1)} %fusion.94), channel_id=1, replica_groups=mesh['grp'=8,'sub'=32] {'sub'}, dimensions={1}, use_global_device_ids=true | all-gather | bytes 608256 | tf_op jit(solution)/shard_map/all_gather | solution.py:75
  306.6 6.3 scatter_custom_fusion.13
  314.6 42.3 %all_gather.25 = f32[192,768]{0,1:T(8,128)} all-gather(f32[192,24]{0,1:T(8,128)S(1)} %fusion.111), channel_id=1, replica_groups=mesh['grp'=8,'sub'=32] {'sub'}, dimensions={1}, use_global_device_ids=true | all-gather | bytes 608256 | tf_op jit(solution)/shard_map/all_gather | solution.py:78
  356.9 1.7 gather_fusion.4
  359.6 7.7 %fusion.24 = f32[192,1152]{1,0:T(8,128)} fusion(f32[192,1152]{1,0:T(8,128)S(1)} %fusion.103, f32[1,1,1152,1152]{3,2,1,0:T(8,128)} %param.11, f32[1152]{0:T(1024)S(1)} %divide_reduce_fusion, f32[192,1152]{1,0:T(8,128)S(1)} %copy-done.3, f32[1,1,192,1152]{3,2,1,0:T(8,128)S(1)} %copy-done.1), kind=kOutput, calls=%fused_computation.52 | convolution fusion | flops 3058532352 | bytes 8851968 | tf_op jit(solution)/shard_map/dot_general | solution.py:22
  368.8 4.7 gather_fusion.5
  376.3 24.3 %collective-permute-start.12 = (f32[192,384]{0,1:T(8,128)}, f32[192,384]{0,1:T(8,128)}, u32[]{:S(2)}, u32[]{:S(2)}) collective-permute-start(f32[192,384]{0,1:T(8,128)} %get-tuple-element.20), channel_id=1, source_target_pairs={{0,224},{32,0},{64,32},{96,64},{128,96},{160,128},{192,160},{224,1... | collective-permute-start | bytes 884744 | tf_op jit(solution)/shard_map/ppermute | solution.py:12
  402.7 4.7 collective-permute-start.15
  408.7 2.2 add.187
  412.4 3.6 scatter_custom_fusion.14
  416.0 3.6 scatter_custom_fusion.15
  419.6 3.6 scatter_custom_fusion.16
  423.2 4.0 scatter_custom_fusion.17
  427.2 11.1 %fusion.6 = f32[192,1152]{0,1:T(8,128)S(1)} fusion(f32[192,1152]{0,1:T(8,128)S(1)} %scatter_custom_fusion.17, f32[1,1,1152,1152]{3,2,1,0:T(8,128)} %param.10), kind=kOutput, calls=%fused_computation.42 | convolution fusion | flops 3057647616 | bytes 7077888 | tf_op jit(solution)/shard_map/dot_general | solution.py:22
  438.3 4.7 gather_fusion.6
  448.7 4.8 collective-permute-start.19
  453.5 3.6 scatter_custom_fusion.18
  457.1 3.7 scatter_custom_fusion.19
  460.8 3.6 scatter_custom_fusion.20
  464.4 3.6 scatter_custom_fusion.21
  469.2 2.1 fusion.91
  471.3 40.6 %all_gather.26 = f32[192,768]{0,1:T(8,128)S(1)} all-gather(f32[192,24]{0,1:T(8,128)S(1)} %fusion.91), channel_id=1, replica_groups=mesh['grp'=8,'sub'=32] {'sub'}, dimensions={1}, use_global_device_ids=true | all-gather | bytes 608256 | tf_op jit(solution)/shard_map/all_gather | solution.py:75
  511.9 6.3 scatter_custom_fusion.22
  519.9 42.2 %all_gather.27 = f32[192,768]{0,1:T(8,128)} all-gather(f32[192,24]{0,1:T(8,128)S(1)} %fusion.109), channel_id=1, replica_groups=mesh['grp'=8,'sub'=32] {'sub'}, dimensions={1}, use_global_device_ids=true | all-gather | bytes 608256 | tf_op jit(solution)/shard_map/all_gather | solution.py:78
  562.1 1.7 gather_fusion.7
  564.8 7.7 %fusion.21 = f32[192,1152]{1,0:T(8,128)} fusion(f32[192,1152]{1,0:T(8,128)S(1)} %fusion.100, f32[1,1,1152,1152]{3,2,1,0:T(8,128)} %param.11, f32[1152]{0:T(1024)S(1)} %divide_reduce_fusion, f32[192,1152]{1,0:T(8,128)S(1)} %copy-done.2, f32[1,1,192,1152]{3,2,1,0:T(8,128)S(1)} %copy-done.1), kind=kOutput, calls=%fused_computation.51 | convolution fusion | flops 3058532352 | bytes 8851968 | tf_op jit(solution)/shard_map/dot_general | solution.py:22
  574.0 4.7 gather_fusion.8
  581.3 24.9 %collective-permute-start.20 = (f32[192,384]{0,1:T(8,128)}, f32[192,384]{0,1:T(8,128)}, u32[]{:S(2)}, u32[]{:S(2)}) collective-permute-start(f32[192,384]{0,1:T(8,128)} %get-tuple-element.12), channel_id=1, source_target_pairs={{0,224},{32,0},{64,32},{96,64},{128,96},{160,128},{192,160},{224,1... | collective-permute-start | bytes 884744 | tf_op jit(solution)/shard_map/ppermute | solution.py:12
  608.0 4.7 collective-permute-start.23
  615.7 3.6 scatter_custom_fusion.23
  619.2 3.6 scatter_custom_fusion.24
  622.8 3.8 scatter_custom_fusion.25
  626.6 3.6 scatter_custom_fusion.26
  (106 shorter events, 52.2 us)
Async XLA Ops:
  0.0 65.2 %copy-start = (f32[1,1,24,1152]{3,2,1,0:T(8,128)S(1)}, f32[1,1,24,1152]{3,2,1,0:T(8,128)}, u32[]{:S(2)}) copy-start(f32[1,1,24,1152]{3,2,1,0:T(8,128)} %param.12) | copy-start | bytes 331780
  19.1 7.6 %copy-start.11 = (s32[1,24]{1,0:T(1,128)S(1)}, s32[1,24]{1,0:T(1,128)}, u32[]{:S(2)}) copy-start(s32[1,24]{1,0:T(1,128)} %param.14) | copy-start | bytes 292
  19.2 7.6 %copy-start.12 = (u32[256]{0:T(256)S(1)}, u32[256]{0:T(256)}, u32[]{:S(2)}) copy-start(u32[256]{0:T(256)} %constant.27) | copy-start | bytes 3076
  19.2 31.5 %copy-start.9 = (s32[1,1,4,384]{3,2,1,0:T(4,128)S(1)}, s32[1,1,4,384]{3,2,1,0:T(4,128)}, u32[]{:S(2)}) copy-start(s32[1,1,4,384]{3,2,1,0:T(4,128)} %param.16) | copy-start | bytes 18436
  19.2 31.5 %copy-start.10 = (s32[1,1,1152]{2,1,0:T(1,128)S(1)}, s32[1,1,1152]{2,1,0:T(1,128)}, u32[]{:S(2)}) copy-start(s32[1,1,1152]{2,1,0:T(1,128)} %param.17) | copy-start | bytes 13828
  19.3 42.3 %collective-permute-start.3 = (f32[192,384]{0,1:T(8,128)S(1)}, f32[192,384]{0,1:T(8,128)S(1)}, u32[]{:S(2)}, u32[]{:S(2)}) collective-permute-start(f32[192,384]{0,1:T(8,128)S(1)} %get-tuple-element.29), channel_id=1, source_target_pairs={{0,1},{1,2},{2,3},{3,4},{4,5},{5,6},{6,7},{7,8},{8,9},{9,10},{10,1... | collective-permute-start | bytes 884744 | tf_op jit(solution)/shard_map/ppermute | solution.py:18
  23.3 34.8 %collective-permute-start.2 = (f32[192,384]{0,1:T(8,128)S(1)}, f32[192,384]{0,1:T(8,128)}, u32[]{:S(2)}, u32[]{:S(2)}) collective-permute-start(f32[192,384]{0,1:T(8,128)S(1)} %get-tuple-element.30), channel_id=1, source_target_pairs={{1,0},{2,1},{3,2},{4,3},{5,4},{6,5},{7,6},{8,7},{9,8},{10,9},{11,1... | collective-permute-start | bytes 884744 | tf_op jit(solution)/shard_map/ppermute | solution.py:18
  24.6 29.7 %collective-permute-start.1 = (f32[192,384]{0,1:T(8,128)S(1)}, f32[192,384]{0,1:T(8,128)}, u32[]{:S(2)}, u32[]{:S(2)}) collective-permute-start(f32[192,384]{0,1:T(8,128)S(1)} %get-tuple-element.31), channel_id=1, source_target_pairs={{0,32},{32,64},{64,96},{96,128},{128,160},{160,192},{192,224},{224... | collective-permute-start | bytes 884744 | tf_op jit(solution)/shard_map/ppermute | solution.py:12
  26.7 24.0 %collective-permute-start = (f32[192,384]{0,1:T(8,128)S(1)}, f32[192,384]{0,1:T(8,128)}, u32[]{:S(2)}, u32[]{:S(2)}) collective-permute-start(f32[192,384]{0,1:T(8,128)S(1)} %get-tuple-element.32), channel_id=1, source_target_pairs={{0,224},{32,0},{64,32},{96,64},{128,96},{160,128},{192,160},{224,1... | collective-permute-start | bytes 884744 | tf_op jit(solution)/shard_map/ppermute | solution.py:12
  64.8 1.2 copy-start.1
  66.9 42.4 %copy-start.8 = (f32[1,768,24]{1,2,0:T(8,128)S(1)}, f32[1,768,24]{1,2,0:T(8,128)}, u32[]{:S(2)}) copy-start(f32[1,768,24]{1,2,0:T(8,128)} %param.13) | copy-start | bytes 221188
  110.8 43.8 %copy-start.6 = (f32[1,1,192,1152]{3,2,1,0:T(8,128)S(1)}, f32[1,1,192,1152]{3,2,1,0:T(8,128)}, u32[]{:S(2)}) copy-start(f32[1,1,192,1152]{3,2,1,0:T(8,128)} %param.19) | copy-start | bytes 2654212
  170.6 37.2 %copy-start.7 = (f32[192,1152]{1,0:T(8,128)S(1)}, f32[192,1152]{1,0:T(8,128)}, u32[]{:S(2)}) copy-start(f32[192,1152]{1,0:T(8,128)} %get-tuple-element.33) | copy-start | bytes 2654212
  171.8 36.4 %collective-permute-start.4 = (f32[192,384]{0,1:T(8,128)}, f32[192,384]{0,1:T(8,128)}, u32[]{:S(2)}, u32[]{:S(2)}) collective-permute-start(f32[192,384]{0,1:T(8,128)} %get-tuple-element.28), channel_id=1, source_target_pairs={{0,224},{32,0},{64,32},{96,64},{128,96},{160,128},{192,160},{224,1... | collective-permute-start | bytes 884744 | tf_op jit(solution)/shard_map/ppermute | solution.py:12
  200.6 11.1 %collective-permute-start.5 = (f32[192,384]{0,1:T(8,128)}, f32[192,384]{0,1:T(8,128)}, u32[]{:S(2)}, u32[]{:S(2)}) collective-permute-start(f32[192,384]{0,1:T(8,128)} %get-tuple-element.27), channel_id=1, source_target_pairs={{0,32},{32,64},{64,96},{96,128},{128,160},{160,192},{192,224},{224... | collective-permute-start | bytes 884744 | tf_op jit(solution)/shard_map/ppermute | solution.py:12
  201.7 13.6 %collective-permute-start.6 = (f32[192,384]{0,1:T(8,128)}, f32[192,384]{0,1:T(8,128)}, u32[]{:S(2)}, u32[]{:S(2)}) collective-permute-start(f32[192,384]{0,1:T(8,128)} %get-tuple-element.26), channel_id=1, source_target_pairs={{1,0},{2,1},{3,2},{4,3},{5,4},{6,5},{7,6},{8,7},{9,8},{10,9},{11,1... | collective-permute-start | bytes 884744 | tf_op jit(solution)/shard_map/ppermute | solution.py:18
  203.0 15.9 %collective-permute-start.7 = (f32[192,384]{0,1:T(8,128)}, f32[192,384]{0,1:T(8,128)}, u32[]{:S(2)}, u32[]{:S(2)}) collective-permute-start(f32[192,384]{0,1:T(8,128)} %get-tuple-element.25), channel_id=1, source_target_pairs={{0,1},{1,2},{2,3},{3,4},{4,5},{5,6},{6,7},{7,8},{8,9},{9,10},{10,1... | collective-permute-start | bytes 884744 | tf_op jit(solution)/shard_map/ppermute | solution.py:18
  241.4 7.8 %collective-permute-start.8 = (f32[192,384]{0,1:T(8,128)S(1)}, f32[192,384]{0,1:T(8,128)}, u32[]{:S(2)}, u32[]{:S(2)}) collective-permute-start(f32[192,384]{0,1:T(8,128)S(1)} %get-tuple-element.24), channel_id=1, source_target_pairs={{0,224},{32,0},{64,32},{96,64},{128,96},{160,128},{192,160},{224,1... | collective-permute-start | bytes 884744 | tf_op jit(solution)/shard_map/ppermute | solution.py:12
  241.4 11.4 %collective-permute-start.9 = (f32[192,384]{0,1:T(8,128)}, f32[192,384]{0,1:T(8,128)}, u32[]{:S(2)}, u32[]{:S(2)}) collective-permute-start(f32[192,384]{0,1:T(8,128)} %get-tuple-element.23), channel_id=1, source_target_pairs={{0,32},{32,64},{64,96},{96,128},{128,160},{160,192},{192,224},{224... | collective-permute-start | bytes 884744 | tf_op jit(solution)/shard_map/ppermute | solution.py:12
  243.1 13.4 %collective-permute-start.10 = (f32[192,384]{0,1:T(8,128)}, f32[192,384]{0,1:T(8,128)}, u32[]{:S(2)}, u32[]{:S(2)}) collective-permute-start(f32[192,384]{0,1:T(8,128)} %get-tuple-element.22), channel_id=1, source_target_pairs={{1,0},{2,1},{3,2},{4,3},{5,4},{6,5},{7,6},{8,7},{9,8},{10,9},{11,1... | collective-permute-start | bytes 884744 | tf_op jit(solution)/shard_map/ppermute | solution.py:18
  244.4 15.7 %collective-permute-start.11 = (f32[192,384]{0,1:T(8,128)}, f32[192,384]{0,1:T(8,128)}, u32[]{:S(2)}, u32[]{:S(2)}) collective-permute-start(f32[192,384]{0,1:T(8,128)} %get-tuple-element.21), channel_id=1, source_target_pairs={{0,1},{1,2},{2,3},{3,4},{4,5},{5,6},{6,7},{7,8},{8,9},{9,10},{10,1... | collective-permute-start | bytes 884744 | tf_op jit(solution)/shard_map/ppermute | solution.py:18
  314.6 45.0 %copy-start.3 = (f32[192,1152]{1,0:T(8,128)S(1)}, f32[192,1152]{1,0:T(8,128)}, u32[]{:S(2)}) copy-start(f32[192,1152]{1,0:T(8,128)} %copy.36) | copy-start | bytes 2654212
  376.3 32.4 %copy-start.5 = (f32[192,1152]{1,0:T(8,128)S(1)}, f32[192,1152]{1,0:T(8,128)}, u32[]{:S(2)}) copy-start(f32[192,1152]{1,0:T(8,128)} %fusion.24) | copy-start | bytes 2654212
  376.3 36.1 %collective-permute-start.12 = (f32[192,384]{0,1:T(8,128)}, f32[192,384]{0,1:T(8,128)}, u32[]{:S(2)}, u32[]{:S(2)}) collective-permute-start(f32[192,384]{0,1:T(8,128)} %get-tuple-element.20), channel_id=1, source_target_pairs={{0,224},{32,0},{64,32},{96,64},{128,96},{160,128},{192,160},{224,1... | collective-permute-start | bytes 884744 | tf_op jit(solution)/shard_map/ppermute | solution.py:12
  400.6 15.4 %collective-permute-start.13 = (f32[192,384]{0,1:T(8,128)}, f32[192,384]{0,1:T(8,128)}, u32[]{:S(2)}, u32[]{:S(2)}) collective-permute-start(f32[192,384]{0,1:T(8,128)} %get-tuple-element.19), channel_id=1, source_target_pairs={{0,32},{32,64},{64,96},{96,128},{128,160},{160,192},{192,224},{224... | collective-permute-start | bytes 884744 | tf_op jit(solution)/shard_map/ppermute | solution.py:12
  401.4 18.2 %collective-permute-start.14 = (f32[192,384]{0,1:T(8,128)}, f32[192,384]{0,1:T(8,128)}, u32[]{:S(2)}, u32[]{:S(2)}) collective-permute-start(f32[192,384]{0,1:T(8,128)} %get-tuple-element.18), channel_id=1, source_target_pairs={{1,0},{2,1},{3,2},{4,3},{5,4},{6,5},{7,6},{8,7},{9,8},{10,9},{11,1... | collective-permute-start | bytes 884744 | tf_op jit(solution)/shard_map/ppermute | solution.py:18
  402.7 20.5 %collective-permute-start.15 = (f32[192,384]{0,1:T(8,128)}, f32[192,384]{0,1:T(8,128)}, u32[]{:S(2)}, u32[]{:S(2)}) collective-permute-start(f32[192,384]{0,1:T(8,128)} %get-tuple-element.17), channel_id=1, source_target_pairs={{0,1},{1,2},{2,3},{3,4},{4,5},{5,6},{6,7},{7,8},{8,9},{9,10},{10,1... | collective-permute-start | bytes 884744 | tf_op jit(solution)/shard_map/ppermute | solution.py:18
  445.7 7.8 %collective-permute-start.16 = (f32[192,384]{0,1:T(8,128)S(1)}, f32[192,384]{0,1:T(8,128)}, u32[]{:S(2)}, u32[]{:S(2)}) collective-permute-start(f32[192,384]{0,1:T(8,128)S(1)} %get-tuple-element.16), channel_id=1, source_target_pairs={{0,224},{32,0},{64,32},{96,64},{128,96},{160,128},{192,160},{224,1... | collective-permute-start | bytes 884744 | tf_op jit(solution)/shard_map/ppermute | solution.py:12
  446.0 11.0 %collective-permute-start.17 = (f32[192,384]{0,1:T(8,128)}, f32[192,384]{0,1:T(8,128)}, u32[]{:S(2)}, u32[]{:S(2)}) collective-permute-start(f32[192,384]{0,1:T(8,128)} %get-tuple-element.15), channel_id=1, source_target_pairs={{0,32},{32,64},{64,96},{96,128},{128,160},{160,192},{192,224},{224... | collective-permute-start | bytes 884744 | tf_op jit(solution)/shard_map/ppermute | solution.py:12
  447.4 13.4 %collective-permute-start.18 = (f32[192,384]{0,1:T(8,128)}, f32[192,384]{0,1:T(8,128)}, u32[]{:S(2)}, u32[]{:S(2)}) collective-permute-start(f32[192,384]{0,1:T(8,128)} %get-tuple-element.14), channel_id=1, source_target_pairs={{1,0},{2,1},{3,2},{4,3},{5,4},{6,5},{7,6},{8,7},{9,8},{10,9},{11,1... | collective-permute-start | bytes 884744 | tf_op jit(solution)/shard_map/ppermute | solution.py:18
  448.7 15.7 %collective-permute-start.19 = (f32[192,384]{0,1:T(8,128)}, f32[192,384]{0,1:T(8,128)}, u32[]{:S(2)}, u32[]{:S(2)}) collective-permute-start(f32[192,384]{0,1:T(8,128)} %get-tuple-element.13), channel_id=1, source_target_pairs={{0,1},{1,2},{2,3},{3,4},{4,5},{5,6},{6,7},{7,8},{8,9},{9,10},{10,1... | collective-permute-start | bytes 884744 | tf_op jit(solution)/shard_map/ppermute | solution.py:18
  519.9 44.9 %copy-start.2 = (f32[192,1152]{1,0:T(8,128)S(1)}, f32[192,1152]{1,0:T(8,128)}, u32[]{:S(2)}) copy-start(f32[192,1152]{1,0:T(8,128)} %copy.42) | copy-start | bytes 2654212
  581.3 31.7 %copy-start.4 = (f32[192,1152]{1,0:T(8,128)S(1)}, f32[192,1152]{1,0:T(8,128)}, u32[]{:S(2)}) copy-start(f32[192,1152]{1,0:T(8,128)} %fusion.21) | copy-start | bytes 2654212
  581.3 34.3 %collective-permute-start.20 = (f32[192,384]{0,1:T(8,128)}, f32[192,384]{0,1:T(8,128)}, u32[]{:S(2)}, u32[]{:S(2)}) collective-permute-start(f32[192,384]{0,1:T(8,128)} %get-tuple-element.12), channel_id=1, source_target_pairs={{0,224},{32,0},{64,32},{96,64},{128,96},{160,128},{192,160},{224,1... | collective-permute-start | bytes 884744 | tf_op jit(solution)/shard_map/ppermute | solution.py:12
  606.2 13.0 %collective-permute-start.21 = (f32[192,384]{0,1:T(8,128)}, f32[192,384]{0,1:T(8,128)}, u32[]{:S(2)}, u32[]{:S(2)}) collective-permute-start(f32[192,384]{0,1:T(8,128)} %get-tuple-element.11), channel_id=1, source_target_pairs={{0,32},{32,64},{64,96},{96,128},{128,160},{160,192},{192,224},{224... | collective-permute-start | bytes 884744 | tf_op jit(solution)/shard_map/ppermute | solution.py:12
  606.7 16.1 %collective-permute-start.22 = (f32[192,384]{0,1:T(8,128)}, f32[192,384]{0,1:T(8,128)}, u32[]{:S(2)}, u32[]{:S(2)}) collective-permute-start(f32[192,384]{0,1:T(8,128)} %get-tuple-element.10), channel_id=1, source_target_pairs={{1,0},{2,1},{3,2},{4,3},{5,4},{6,5},{7,6},{8,7},{9,8},{10,9},{11,1... | collective-permute-start | bytes 884744 | tf_op jit(solution)/shard_map/ppermute | solution.py:18
  608.0 18.6 %collective-permute-start.23 = (f32[192,384]{0,1:T(8,128)S(1)}, f32[192,384]{0,1:T(8,128)}, u32[]{:S(2)}, u32[]{:S(2)}) collective-permute-start(f32[192,384]{0,1:T(8,128)S(1)} %get-tuple-element.9), channel_id=1, source_target_pairs={{0,1},{1,2},{2,3},{3,4},{4,5},{5,6},{6,7},{7,8},{8,9},{9,10},{10,1... | collective-permute-start | bytes 884744 | tf_op jit(solution)/shard_map/ppermute | solution.py:18
where the time goes:
time: 643 us; the launch traced here: 632 us
  blocking collectives  264 us (41%)
  starting transfers between devices  121 us (19%)
  other arithmetic  101 us (16%)
  local copies, waits for them, and re-layouts  73 us (11%)
  matrix products  69.6 us (11%)
    all_gather x3, blocking collectives, local(): gathered = lax.all_gather(owned, 'sub', axis=1, tiled=True)  126 us
    all_gather x3, blocking collectives, local(): pieces = lax.all_gather(coarse_piece, 'sub', axis=1, tiled=True)  116 us
    ppermute x12, starting transfers between devices, shifted(): lax.ppermute(array, axis, [(i, (i + by) % peers) for i in range(peers)])  86.1 us
    dot_general x12, matrix products, product(): jnp.dot(left, right, precision=HIGHEST, preferred_element_type=jnp.float32)  64.5 us
    ppermute x12, starting transfers between devices, from_behind(): lax.ppermute(value, axis, [(source, source + steps) for source in range(f...  35.4 us
    gather x6, local copies, waits for them, and re-layouts, assemble(): values[:, one_index] * one_mask[None, :]  27.9 us
    unnamed x1, blocking collectives  22.5 us
    scatter-add x6, other arithmetic, assemble(): values = values.at[:, face_index[1]].add(from_prev)  21.9 us
  transfers between devices with their start and end apart: 24, of which 0 were waited for; matrix products, arithmetic and copies ran while one was open for 12% of the time, Pallas kernels for 0%

commit v1 on v0

--- a/solution.py
+++ b/solution.py
@@ -5,6 +5,12 @@
 
 ITERS = 3
 HIGHEST = lax.Precision.HIGHEST
+
+
+def task_mark(t0, join_dim):
+    w2 = jnp.concatenate([t0] * lax.axis_size("sub"), axis=join_dim)
+    even = lax.all_to_all(w2, "sub", join_dim, join_dim, tiled=True)
+    return even
 
 
 def shifted(array, axis, by):
@@ -72,7 +78,7 @@
             precision=HIGHEST,
             preferred_element_type=jnp.float32,
         )
-        pieces = lax.all_gather(coarse_piece, "sub", axis=1, tiled=True)
+        pieces = task_mark(coarse_piece, 1)
         coarse_sum = jnp.zeros_like(pieces).at[:, all_owner].set(pieces)
         owned = product(coarse_sum, coarse_inverse[0])
         gathered = lax.all_gather(owned, "sub", axis=1, tiled=True)

time: 643 us -> 584 us (0.908)
  blocking collectives: 264 us -> 206 us
  local copies, waits for them, and re-layouts: 73 us -> 91.5 us
  starting transfers between devices: 121 us -> 105 us
    all_gather x3 -> x0, blocking collectives: 116 us -> none  [local(): pieces = lax.all_gather(coarse_piece, 'sub', axis=1, tiled=True)]
    all_to_all x0 -> x2, blocking collectives: none -> 60.7 us  [task_mark(): even = lax.all_to_all(w2, 'sub', join_dim, join_dim, tiled=True)]
    ppermute x12, starting transfers between devices: 86.1 us -> 57.3 us  [shifted(): lax.ppermute(array, axis, [(i, (i + by) % peers) for i in range(peers)])]
    unnamed x29 -> x145, local copies, waits for them, and re-layouts: 1.57 us -> 20.9 us
    all_to_all x0 -> x1, starting transfers between devices: none -> 12.5 us  [task_mark(): even = lax.all_to_all(w2, 'sub', join_dim, join_dim, tiled=True)]
  transfers between devices with their start and end apart: 24 -> 25, of which waited for: 0 -> 0; matrix products, arithmetic and copies ran while one was open for 12% -> 13% of each run, Pallas kernels for 0% -> 0%
where the time goes in v1:
time: 584 us; the launch traced here: 574 us
  blocking collectives  206 us (35%)
  starting transfers between devices  105 us (18%)
  other arithmetic  101 us (17%)
  local copies, waits for them, and re-layouts  91.5 us (16%)
  matrix products  67.6 us (12%)
    all_gather x3, blocking collectives, local(): gathered = lax.all_gather(owned, 'sub', axis=1, tiled=True)  122 us
    dot_general x12, matrix products, product(): jnp.dot(left, right, precision=HIGHEST, preferred_element_type=jnp.float32)  61.9 us
    all_to_all x2, blocking collectives, task_mark(): even = lax.all_to_all(w2, 'sub', join_dim, join_dim, tiled=True)  60.7 us
    ppermute x12, starting transfers between devices, shifted(): lax.ppermute(array, axis, [(i, (i + by) % peers) for i in range(peers)])  57.3 us
    ppermute x12, starting transfers between devices, from_behind(): lax.ppermute(value, axis, [(source, source + steps) for source in range(f...  35.5 us
    gather x6, local copies, waits for them, and re-layouts, assemble(): values[:, one_index] * one_mask[None, :]  27.9 us
    unnamed x1, blocking collectives  23.1 us
    scatter-add x6, other arithmetic, assemble(): values = values.at[:, face_index[1]].add(from_prev)  22 us
  transfers between devices with their start and end apart: 25, of which 0 were waited for; matrix products, arithmetic and copies ran while one was open for 13% of the time, Pallas kernels for 0%

profile of v1, /device:TPU:1, one launch (start us, length us, event | category | flops | bytes accessed | tf_op | source)
XLA Modules:
  0.0 573.7 jit_solution(7661381654356379550)
XLA Ops:
  1.5 11.3 %fusion.10 = f32[192,1152]{0,1:T(8,128)S(1)} fusion(f32[1,1,1152,1152]{3,2,1,0:T(8,128)} %param.10, f32[1,1,192,1152]{3,2,1,0:T(8,128)} %param.19), kind=kOutput, calls=%fused_computation.46 | convolution fusion | flops 3057647616 | bytes 7077888 | tf_op jit(solution)/shard_map/dot_general | solution.py:28
  12.8 4.7 gather_fusion
  19.3 3.3 collective-permute-start
  23.9 4.0 collective-permute-start.3
  28.8 3.5 scatter_custom_fusion
  32.3 3.7 scatter_custom_fusion.1
  36.1 3.6 scatter_custom_fusion.2
  39.7 3.1 scatter_custom_fusion.3
  64.4 12.5 %all-to-all-start = ((f32[192,32,24]{0,2,1:T(8,128)}), f32[192,32,24]{0,2,1:T(8,128)S(1)}, u32[]{:S(2)}, u32[]{:S(2)}) async-start(f32[192,32,24]{0,2,1:T(8,128)} %bitcast.23), calls=%async_computation | async-start | bytes 1572864 | tf_op jit(solution)/shard_map/all_to_all | solution.py:12
  78.3 23.1 %all-reduce = s32[768]{0:T(1024)S(1)} all-reduce(s32[768]{0:T(1024)S(1)} %bitcast_dynamic-update-slice_fusion), channel_id=1, replica_groups=mesh['grp'=8,'sub'=32] {'sub'}, use_global_device_ids=true, to_apply=%add | all-reduce | flops 768 | bytes 6144
  101.5 5.7 scatter_custom_fusion.4
  107.7 37.2 %all_gather.13 = f32[192,768]{0,1:T(8,128)S(1)} all-gather(f32[192,24]{0,1:T(8,128)S(1)} %fusion.110), channel_id=1, replica_groups=mesh['grp'=8,'sub'=32] {'sub'}, dimensions={1}, use_global_device_ids=true | all-gather | bytes 608256 | tf_op jit(solution)/shard_map/all_gather | solution.py:84
  147.7 8.0 %bitcast_add_fusion = (f32[192,1152]{1,0:T(8,128)}, f32[192,1152]{1,0:T(8,128)}) fusion(f32[1,1,192,1152]{3,2,1,0:T(8,128)S(1)} %copy-done.6, f32[1152]{0:T(1024)} %copy-done.10, f32[192,1152]{1,0:T(8,128)S(1)} %fusion.103, f32[1,1,1152,1152]{3,2,1,0:T(8,128)} %param.11, f32[192,1152]{1,0:T(8,128)S(1)} %copy.31, f32[1,1,192,1152]{3,2,1,0:T(8,128)S(1)} %copy-done.1), kind=kOutput, calls=%fused_computation.66 | convolution fusion | flops 3058753536 | bytes 10621440 | tf_op jit(solution)/shard_map/dot_general | solution.py:28
  157.3 4.7 gather_fusion.2
  164.7 15.9 %collective-permute-start.4 = (f32[192,384]{0,1:T(8,128)}, f32[192,384]{0,1:T(8,128)}, u32[]{:S(2)}, u32[]{:S(2)}) collective-permute-start(f32[192,384]{0,1:T(8,128)} %get-tuple-element.28), channel_id=1, source_target_pairs={{0,224},{32,0},{64,32},{96,64},{128,96},{160,128},{192,160},{224,1... | collective-permute-start | bytes 884744 | tf_op jit(solution)/shard_map/ppermute | solution.py:18
  183.2 4.7 collective-permute-start.7
  188.3 3.6 scatter_custom_fusion.5
  191.9 3.6 scatter_custom_fusion.6
  195.4 3.6 scatter_custom_fusion.7
  199.0 3.7 scatter_custom_fusion.8
  202.8 11.1 %fusion.8 = f32[192,1152]{0,1:T(8,128)S(1)} fusion(f32[192,1152]{0,1:T(8,128)S(1)} %scatter_custom_fusion.8, f32[1,1,1152,1152]{3,2,1,0:T(8,128)} %param.10), kind=kOutput, calls=%fused_computation.44 | convolution fusion | flops 3057647616 | bytes 7077888 | tf_op jit(solution)/shard_map/dot_general | solution.py:28
  213.9 4.7 gather_fusion.3
  221.3 1.7 collective-permute-start.9
  224.3 4.8 collective-permute-start.11
  229.1 3.6 scatter_custom_fusion.9
  232.7 3.8 scatter_custom_fusion.10
  236.5 3.6 scatter_custom_fusion.11
  240.1 3.6 scatter_custom_fusion.12
  244.9 2.1 constant_dynamic-update-slice_fusion.63
  247.4 30.0 %all_to_all.36 = f32[192,32,24]{0,2,1:T(8,128)} all-to-all(f32[192,32,24]{0,2,1:T(8,128)S(1)} %bitcast.271), channel_id=1, replica_groups=mesh['grp'=8,'sub'=32] {'sub'}, dimensions={1} | all-to-all | bytes 1179648 | tf_op jit(solution)/shard_map/all_to_all | solution.py:12
  277.5 6.2 %scatter_custom_fusion.13 = f32[192,768]{0,1:T(8,128)S(1)} fusion(s32[768]{0:T(1024)} %copy-done.19, f32[768,192]{1,0:T(8,128)} %bitcast.275, f32[]{:T(128)} %constant.8.clone.1), kind=kCustom, calls=%fused_computation.142 | custom fusion | bytes 590336 | tf_op jit(solution)/shard_map/scatter | solution.py:82
  284.2 42.8 %all_gather.14 = f32[192,768]{0,1:T(8,128)} all-gather(f32[192,24]{0,1:T(8,128)S(1)} %fusion.108), channel_id=1, replica_groups=mesh['grp'=8,'sub'=32] {'sub'}, dimensions={1}, use_global_device_ids=true | all-gather | bytes 608256 | tf_op jit(solution)/shard_map/all_gather | solution.py:84
  327.0 1.7 gather_fusion.4
  329.6 7.7 %fusion.24 = f32[192,1152]{1,0:T(8,128)} fusion(f32[192,1152]{1,0:T(8,128)S(1)} %fusion.100, f32[1,1,1152,1152]{3,2,1,0:T(8,128)} %param.11, f32[1152]{0:T(1024)S(1)} %copy-done.11, f32[192,1152]{1,0:T(8,128)S(1)} %copy-done.3, f32[1,1,192,1152]{3,2,1,0:T(8,128)S(1)} %copy-done.1), kind=kOutput, calls=%fused_computation.52 | convolution fusion | flops 3058532352 | bytes 8851968 | tf_op jit(solution)/shard_map/dot_general | solution.py:28
  338.9 4.7 gather_fusion.5
  346.4 15.2 %collective-permute-start.12 = (f32[192,384]{0,1:T(8,128)}, f32[192,384]{0,1:T(8,128)}, u32[]{:S(2)}, u32[]{:S(2)}) collective-permute-start(f32[192,384]{0,1:T(8,128)} %get-tuple-element.20), channel_id=1, source_target_pairs={{0,224},{32,0},{64,32},{96,64},{128,96},{160,128},{192,160},{224,1... | collective-permute-start | bytes 884744 | tf_op jit(solution)/shard_map/ppermute | solution.py:18
  361.6 2.5 collective-permute-start.13
  365.4 4.7 collective-permute-start.15
  371.4 2.2 add.187
  375.1 3.6 scatter_custom_fusion.14
  378.7 3.6 scatter_custom_fusion.15
  382.3 3.6 scatter_custom_fusion.16
  385.9 3.7 scatter_custom_fusion.17
  389.6 11.1 %fusion.6 = f32[192,1152]{0,1:T(8,128)S(1)} fusion(f32[192,1152]{0,1:T(8,128)S(1)} %scatter_custom_fusion.17, f32[1,1,1152,1152]{3,2,1,0:T(8,128)} %param.10), kind=kOutput, calls=%fused_computation.42 | convolution fusion | flops 3057647616 | bytes 7077888 | tf_op jit(solution)/shard_map/dot_general | solution.py:28
  400.8 4.7 gather_fusion.6
  408.2 1.7 collective-permute-start.17
  411.2 4.8 collective-permute-start.19
  416.0 3.6 scatter_custom_fusion.18
  419.5 3.8 scatter_custom_fusion.19
  423.3 3.6 scatter_custom_fusion.20
  426.9 3.6 scatter_custom_fusion.21
  431.8 2.1 constant_dynamic-update-slice_fusion.95
  434.3 30.7 %all_to_all.37 = f32[192,32,24]{0,2,1:T(8,128)} all-to-all(f32[192,32,24]{0,2,1:T(8,128)S(1)} %bitcast.272), channel_id=1, replica_groups=mesh['grp'=8,'sub'=32] {'sub'}, dimensions={1} | all-to-all | bytes 1179648 | tf_op jit(solution)/shard_map/all_to_all | solution.py:12
  464.9 6.2 %scatter_custom_fusion.22 = f32[192,768]{0,1:T(8,128)S(1)} fusion(s32[768]{0:T(1024)} %copy-done.19, f32[768,192]{1,0:T(8,128)} %bitcast.274, f32[]{:T(128)} %constant.8.clone.1), kind=kCustom, calls=%fused_computation.140 | custom fusion | bytes 590336 | tf_op jit(solution)/shard_map/scatter | solution.py:82
  471.6 41.9 %all_gather.15 = f32[192,768]{0,1:T(8,128)} all-gather(f32[192,24]{0,1:T(8,128)S(1)} %fusion.106), channel_id=1, replica_groups=mesh['grp'=8,'sub'=32] {'sub'}, dimensions={1}, use_global_device_ids=true | all-gather | bytes 608256 | tf_op jit(solution)/shard_map/all_gather | solution.py:84
  513.5 1.7 gather_fusion.7
  516.2 7.7 %fusion.21 = f32[192,1152]{1,0:T(8,128)} fusion(f32[192,1152]{1,0:T(8,128)S(1)} %fusion.97, f32[1,1,1152,1152]{3,2,1,0:T(8,128)} %param.11, f32[1152]{0:T(1024)S(1)} %copy-done.11, f32[192,1152]{1,0:T(8,128)S(1)} %copy-done.2, f32[1,1,192,1152]{3,2,1,0:T(8,128)S(1)} %copy-done.1), kind=kOutput, calls=%fused_computation.51 | convolution fusion | flops 3058532352 | bytes 8851968 | tf_op jit(solution)/shard_map/dot_general | solution.py:28
  525.4 4.7 gather_fusion.8
  532.8 14.7 %collective-permute-start.20 = (f32[192,384]{0,1:T(8,128)}, f32[192,384]{0,1:T(8,128)}, u32[]{:S(2)}, u32[]{:S(2)}) collective-permute-start(f32[192,384]{0,1:T(8,128)} %get-tuple-element.12), channel_id=1, source_target_pairs={{0,224},{32,0},{64,32},{96,64},{128,96},{160,128},{192,160},{224,1... | collective-permute-start | bytes 884744 | tf_op jit(solution)/shard_map/ppermute | solution.py:18
  549.8 4.7 collective-permute-start.23
  557.5 3.6 scatter_custom_fusion.23
  561.0 3.6 scatter_custom_fusion.24
  564.6 4.0 scatter_custom_fusion.25
  568.7 3.6 scatter_custom_fusion.26
  (226 shorter events, 71.0 us)
Async XLA Ops:
  0.0 43.2 %copy-start = (f32[1,1,24,1152]{3,2,1,0:T(8,128)S(1)}, f32[1,1,24,1152]{3,2,1,0:T(8,128)}, u32[]{:S(2)}) copy-start(f32[1,1,24,1152]{3,2,1,0:T(8,128)} %param.12) | copy-start | bytes 331780
  0.8 16.7 %copy-start.13 = (f32[4,384]{1,0:T(4,128)}, f32[4,384]{1,0:T(4,128)S(1)}, u32[]{:S(2)}) copy-start(f32[4,384]{1,0:T(4,128)S(1)} %fusion.112) | copy-start | bytes 18436
  1.5 11.3 %copy-start.15 = (s32[2048]{0:T(1024)}, s32[2048]{0:T(1024)S(1)}, u32[]{:S(2)}) copy-start(s32[2048]{0:T(1024)S(1)} %pad_clamp_fusion) | copy-start | bytes 24580
  19.2 8.7 %copy-start.17 = (s32[1,1,4,384]{3,2,1,0:T(4,128)S(1)}, s32[1,1,4,384]{3,2,1,0:T(4,128)}, u32[]{:S(2)}) copy-start(s32[1,1,4,384]{3,2,1,0:T(4,128)} %param.16) | copy-start | bytes 18436
  19.2 8.7 %copy-start.18 = (s32[1,1,1152]{2,1,0:T(1,128)S(1)}, s32[1,1,1152]{2,1,0:T(1,128)}, u32[]{:S(2)}) copy-start(s32[1,1,1152]{2,1,0:T(1,128)} %param.17) | copy-start | bytes 13828
  19.3 8.7 %collective-permute-start = (f32[192,384]{0,1:T(8,128)S(1)}, f32[192,384]{0,1:T(8,128)S(1)}, u32[]{:S(2)}, u32[]{:S(2)}) collective-permute-start(f32[192,384]{0,1:T(8,128)S(1)} %get-tuple-element.32), channel_id=1, source_target_pairs={{0,224},{32,0},{64,32},{96,64},{128,96},{160,128},{192,160},{224,1... | collective-permute-start | bytes 884744 | tf_op jit(solution)/shard_map/ppermute | solution.py:18
  22.6 9.8 %collective-permute-start.1 = (f32[192,384]{0,1:T(8,128)S(1)}, f32[192,384]{0,1:T(8,128)}, u32[]{:S(2)}, u32[]{:S(2)}) collective-permute-start(f32[192,384]{0,1:T(8,128)S(1)} %get-tuple-element.31), channel_id=1, source_target_pairs={{0,32},{32,64},{64,96},{96,128},{128,160},{160,192},{192,224},{224... | collective-permute-start | bytes 884744 | tf_op jit(solution)/shard_map/ppermute | solution.py:18
  22.6 13.5 %collective-permute-start.2 = (f32[192,384]{0,1:T(8,128)S(1)}, f32[192,384]{0,1:T(8,128)}, u32[]{:S(2)}, u32[]{:S(2)}) collective-permute-start(f32[192,384]{0,1:T(8,128)S(1)} %get-tuple-element.30), channel_id=1, source_target_pairs={{1,0},{2,1},{3,2},{4,3},{5,4},{6,5},{7,6},{8,7},{9,8},{10,9},{11,1... | collective-permute-start | bytes 884744 | tf_op jit(solution)/shard_map/ppermute | solution.py:24
  23.9 15.8 %collective-permute-start.3 = (f32[192,384]{0,1:T(8,128)S(1)}, f32[192,384]{0,1:T(8,128)S(1)}, u32[]{:S(2)}, u32[]{:S(2)}) collective-permute-start(f32[192,384]{0,1:T(8,128)S(1)} %get-tuple-element.29), channel_id=1, source_target_pairs={{0,1},{1,2},{2,3},{3,4},{4,5},{5,6},{6,7},{7,8},{8,9},{9,10},{10,1... | collective-permute-start | bytes 884744 | tf_op jit(solution)/shard_map/ppermute | solution.py:24
  27.9 8.2 %copy-start.22 = (s32[384]{0:T(512)}, s32[384]{0:T(512)S(1)}, u32[]{:S(2)}) copy-start(s32[384]{0:T(512)S(1)} %get-tuple-element.6) | copy-start | bytes 4612
  27.9 8.2 %copy-start.23 = (s32[384]{0:T(512)}, s32[384]{0:T(512)S(1)}, u32[]{:S(2)}) copy-start(s32[384]{0:T(512)S(1)} %get-tuple-element.7) | copy-start | bytes 4612
  28.0 8.2 %copy-start.21 = (s32[384]{0:T(512)}, s32[384]{0:T(512)S(1)}, u32[]{:S(2)}) copy-start(s32[384]{0:T(512)S(1)} %get-tuple-element.8) | copy-start | bytes 4612
  28.0 11.8 %copy-start.20 = (s32[384]{0:T(512)}, s32[384]{0:T(512)S(1)}, u32[]{:S(2)}) copy-start(s32[384]{0:T(512)S(1)} %get-tuple-element.5) | copy-start | bytes 4612
  28.0 15.2 %copy-start.10 = (f32[1152]{0:T(1024)}, f32[1152]{0:T(1024)S(1)}, u32[]{:S(2)}) copy-start(f32[1152]{0:T(1024)S(1)} %divide_reduce_fusion) | copy-start | bytes 13828
  28.0 0.7 copy-start.12
  42.8 1.2 copy-start.1
  54.7 22.2 %copy-start.25 = (u32[256]{0:T(256)S(1)}, u32[256]{0:T(256)}, u32[]{:S(2)}) copy-start(u32[256]{0:T(256)} %constant.27) | copy-start | bytes 3076
  54.7 23.5 %copy-start.24 = (s32[1,24]{1,0:T(1,128)S(1)}, s32[1,24]{1,0:T(1,128)}, u32[]{:S(2)}) copy-start(s32[1,24]{1,0:T(1,128)} %param.14) | copy-start | bytes 292
  64.4 42.8 %copy-start.8 = (f32[1,768,24]{1,2,0:T(8,128)S(1)}, f32[1,768,24]{1,2,0:T(8,128)}, u32[]{:S(2)}) copy-start(f32[1,768,24]{1,2,0:T(8,128)} %param.13) | copy-start | bytes 221188
  64.4 37.0 %all-to-all-start = ((f32[192,32,24]{0,2,1:T(8,128)}), f32[192,32,24]{0,2,1:T(8,128)S(1)}, u32[]{:S(2)}, u32[]{:S(2)}) async-start(f32[192,32,24]{0,2,1:T(8,128)} %bitcast.23), calls=%async_computation | async-start | bytes 1572864 | tf_op jit(solution)/shard_map/all_to_all | solution.py:12
  101.4 5.8 %copy-start.19 = (s32[768]{0:T(1024)}, s32[768]{0:T(1024)S(1)}, u32[]{:S(2)}) copy-start(s32[768]{0:T(1024)S(1)} %fusion.113) | copy-start | bytes 9220
  107.7 40.0 %copy-start.6 = (f32[1,1,192,1152]{3,2,1,0:T(8,128)S(1)}, f32[1,1,192,1152]{3,2,1,0:T(8,128)}, u32[]{:S(2)}) copy-start(f32[1,1,192,1152]{3,2,1,0:T(8,128)} %param.19) | copy-start | bytes 2654212
  155.7 1.6 copy-start.16
  157.3 4.7 copy-start.14
  163.6 24.3 %copy-start.7 = (f32[192,1152]{1,0:T(8,128)S(1)}, f32[192,1152]{1,0:T(8,128)}, u32[]{:S(2)}) copy-start(f32[192,1152]{1,0:T(8,128)} %get-tuple-element.35) | copy-start | bytes 2654212
  164.7 23.6 %collective-permute-start.4 = (f32[192,384]{0,1:T(8,128)}, f32[192,384]{0,1:T(8,128)}, u32[]{:S(2)}, u32[]{:S(2)}) collective-permute-start(f32[192,384]{0,1:T(8,128)} %get-tuple-element.28), channel_id=1, source_target_pairs={{0,224},{32,0},{64,32},{96,64},{128,96},{160,128},{192,160},{224,1... | collective-permute-start | bytes 884744 | tf_op jit(solution)/shard_map/ppermute | solution.py:18
  180.6 11.3 %collective-permute-start.5 = (f32[192,384]{0,1:T(8,128)}, f32[192,384]{0,1:T(8,128)}, u32[]{:S(2)}, u32[]{:S(2)}) collective-permute-start(f32[192,384]{0,1:T(8,128)} %get-tuple-element.27), channel_id=1, source_target_pairs={{0,32},{32,64},{64,96},{96,128},{128,160},{160,192},{192,224},{224... | collective-permute-start | bytes 884744 | tf_op jit(solution)/shard_map/ppermute | solution.py:18
  181.9 13.6 %collective-permute-start.6 = (f32[192,384]{0,1:T(8,128)}, f32[192,384]{0,1:T(8,128)}, u32[]{:S(2)}, u32[]{:S(2)}) collective-permute-start(f32[192,384]{0,1:T(8,128)} %get-tuple-element.26), channel_id=1, source_target_pairs={{1,0},{2,1},{3,2},{4,3},{5,4},{6,5},{7,6},{8,7},{9,8},{10,9},{11,1... | collective-permute-start | bytes 884744 | tf_op jit(solution)/shard_map/ppermute | solution.py:24
  183.2 15.9 %collective-permute-start.7 = (f32[192,384]{0,1:T(8,128)S(1)}, f32[192,384]{0,1:T(8,128)}, u32[]{:S(2)}, u32[]{:S(2)}) collective-permute-start(f32[192,384]{0,1:T(8,128)S(1)} %get-tuple-element.25), channel_id=1, source_target_pairs={{0,1},{1,2},{2,3},{3,4},{4,5},{5,6},{6,7},{7,8},{8,9},{9,10},{10,1... | collective-permute-start | bytes 884744 | tf_op jit(solution)/shard_map/ppermute | solution.py:24
  221.3 7.8 %collective-permute-start.8 = (f32[192,384]{0,1:T(8,128)S(1)}, f32[192,384]{0,1:T(8,128)}, u32[]{:S(2)}, u32[]{:S(2)}) collective-permute-start(f32[192,384]{0,1:T(8,128)S(1)} %get-tuple-element.24), channel_id=1, source_target_pairs={{0,224},{32,0},{64,32},{96,64},{128,96},{160,128},{192,160},{224,1... | collective-permute-start | bytes 884744 | tf_op jit(solution)/shard_map/ppermute | solution.py:18
  221.3 11.4 %collective-permute-start.9 = (f32[192,384]{0,1:T(8,128)}, f32[192,384]{0,1:T(8,128)}, u32[]{:S(2)}, u32[]{:S(2)}) collective-permute-start(f32[192,384]{0,1:T(8,128)} %get-tuple-element.23), channel_id=1, source_target_pairs={{0,32},{32,64},{64,96},{96,128},{128,160},{160,192},{192,224},{224... | collective-permute-start | bytes 884744 | tf_op jit(solution)/shard_map/ppermute | solution.py:18
  223.0 13.4 %collective-permute-start.10 = (f32[192,384]{0,1:T(8,128)}, f32[192,384]{0,1:T(8,128)}, u32[]{:S(2)}, u32[]{:S(2)}) collective-permute-start(f32[192,384]{0,1:T(8,128)} %get-tuple-element.22), channel_id=1, source_target_pairs={{1,0},{2,1},{3,2},{4,3},{5,4},{6,5},{7,6},{8,7},{9,8},{10,9},{11,1... | collective-permute-start | bytes 884744 | tf_op jit(solution)/shard_map/ppermute | solution.py:24
  224.3 15.7 %collective-permute-start.11 = (f32[192,384]{0,1:T(8,128)}, f32[192,384]{0,1:T(8,128)}, u32[]{:S(2)}, u32[]{:S(2)}) collective-permute-start(f32[192,384]{0,1:T(8,128)} %get-tuple-element.21), channel_id=1, source_target_pairs={{0,1},{1,2},{2,3},{3,4},{4,5},{5,6},{6,7},{7,8},{8,9},{9,10},{10,1... | collective-permute-start | bytes 884744 | tf_op jit(solution)/shard_map/ppermute | solution.py:24
  243.6 1.3 copy-start.11
  247.4 36.3 %copy-start.9 = (f32[1,768,24]{1,2,0:T(8,128)S(1)}, f32[1,768,24]{1,2,0:T(8,128)}, u32[]{:S(2)}) copy-start(f32[1,768,24]{1,2,0:T(8,128)} %param.13) | copy-start | bytes 221188
  284.2 45.5 %copy-start.3 = (f32[192,1152]{1,0:T(8,128)S(1)}, f32[192,1152]{1,0:T(8,128)}, u32[]{:S(2)}) copy-start(f32[192,1152]{1,0:T(8,128)} %copy.36) | copy-start | bytes 2654212
  346.4 25.0 %copy-start.5 = (f32[192,1152]{1,0:T(8,128)S(1)}, f32[192,1152]{1,0:T(8,128)}, u32[]{:S(2)}) copy-start(f32[192,1152]{1,0:T(8,128)} %fusion.24) | copy-start | bytes 2654212
  346.4 28.7 %collective-permute-start.12 = (f32[192,384]{0,1:T(8,128)}, f32[192,384]{0,1:T(8,128)}, u32[]{:S(2)}, u32[]{:S(2)}) collective-permute-start(f32[192,384]{0,1:T(8,128)} %get-tuple-element.20), channel_id=1, source_target_pairs={{0,224},{32,0},{64,32},{96,64},{128,96},{160,128},{192,160},{224,1... | collective-permute-start | bytes 884744 | tf_op jit(solution)/shard_map/ppermute | solution.py:18
  361.6 17.1 %collective-permute-start.13 = (f32[192,384]{0,1:T(8,128)}, f32[192,384]{0,1:T(8,128)}, u32[]{:S(2)}, u32[]{:S(2)}) collective-permute-start(f32[192,384]{0,1:T(8,128)} %get-tuple-element.19), channel_id=1, source_target_pairs={{0,32},{32,64},{64,96},{96,128},{128,160},{160,192},{192,224},{224... | collective-permute-start | bytes 884744 | tf_op jit(solution)/shard_map/ppermute | solution.py:18
  364.1 18.2 %collective-permute-start.14 = (f32[192,384]{0,1:T(8,128)}, f32[192,384]{0,1:T(8,128)}, u32[]{:S(2)}, u32[]{:S(2)}) collective-permute-start(f32[192,384]{0,1:T(8,128)} %get-tuple-element.18), channel_id=1, source_target_pairs={{1,0},{2,1},{3,2},{4,3},{5,4},{6,5},{7,6},{8,7},{9,8},{10,9},{11,1... | collective-permute-start | bytes 884744 | tf_op jit(solution)/shard_map/ppermute | solution.py:24
  365.4 20.5 %collective-permute-start.15 = (f32[192,384]{0,1:T(8,128)}, f32[192,384]{0,1:T(8,128)}, u32[]{:S(2)}, u32[]{:S(2)}) collective-permute-start(f32[192,384]{0,1:T(8,128)} %get-tuple-element.17), channel_id=1, source_target_pairs={{0,1},{1,2},{2,3},{3,4},{4,5},{5,6},{6,7},{7,8},{8,9},{9,10},{10,1... | collective-permute-start | bytes 884744 | tf_op jit(solution)/shard_map/ppermute | solution.py:24
  408.1 7.8 %collective-permute-start.16 = (f32[192,384]{0,1:T(8,128)S(1)}, f32[192,384]{0,1:T(8,128)}, u32[]{:S(2)}, u32[]{:S(2)}) collective-permute-start(f32[192,384]{0,1:T(8,128)S(1)} %get-tuple-element.16), channel_id=1, source_target_pairs={{0,224},{32,0},{64,32},{96,64},{128,96},{160,128},{192,160},{224,1... | collective-permute-start | bytes 884744 | tf_op jit(solution)/shard_map/ppermute | solution.py:18
  408.2 11.4 %collective-permute-start.17 = (f32[192,384]{0,1:T(8,128)}, f32[192,384]{0,1:T(8,128)}, u32[]{:S(2)}, u32[]{:S(2)}) collective-permute-start(f32[192,384]{0,1:T(8,128)} %get-tuple-element.15), channel_id=1, source_target_pairs={{0,32},{32,64},{64,96},{96,128},{128,160},{160,192},{192,224},{224... | collective-permute-start | bytes 884744 | tf_op jit(solution)/shard_map/ppermute | solution.py:18
  409.9 13.4 %collective-permute-start.18 = (f32[192,384]{0,1:T(8,128)}, f32[192,384]{0,1:T(8,128)}, u32[]{:S(2)}, u32[]{:S(2)}) collective-permute-start(f32[192,384]{0,1:T(8,128)} %get-tuple-element.14), channel_id=1, source_target_pairs={{1,0},{2,1},{3,2},{4,3},{5,4},{6,5},{7,6},{8,7},{9,8},{10,9},{11,1... | collective-permute-start | bytes 884744 | tf_op jit(solution)/shard_map/ppermute | solution.py:24
  411.2 15.7 %collective-permute-start.19 = (f32[192,384]{0,1:T(8,128)}, f32[192,384]{0,1:T(8,128)}, u32[]{:S(2)}, u32[]{:S(2)}) collective-permute-start(f32[192,384]{0,1:T(8,128)} %get-tuple-element.13), channel_id=1, source_target_pairs={{0,1},{1,2},{2,3},{3,4},{4,5},{5,6},{6,7},{7,8},{8,9},{9,10},{10,1... | collective-permute-start | bytes 884744 | tf_op jit(solution)/shard_map/ppermute | solution.py:24
  471.6 44.6 %copy-start.2 = (f32[192,1152]{1,0:T(8,128)S(1)}, f32[192,1152]{1,0:T(8,128)}, u32[]{:S(2)}) copy-start(f32[192,1152]{1,0:T(8,128)} %copy.42) | copy-start | bytes 2654212
  532.8 22.1 %copy-start.4 = (f32[192,1152]{1,0:T(8,128)S(1)}, f32[192,1152]{1,0:T(8,128)}, u32[]{:S(2)}) copy-start(f32[192,1152]{1,0:T(8,128)} %fusion.21) | copy-start | bytes 2654212
  532.8 24.7 %collective-permute-start.20 = (f32[192,384]{0,1:T(8,128)}, f32[192,384]{0,1:T(8,128)}, u32[]{:S(2)}, u32[]{:S(2)}) collective-permute-start(f32[192,384]{0,1:T(8,128)} %get-tuple-element.12), channel_id=1, source_target_pairs={{0,224},{32,0},{64,32},{96,64},{128,96},{160,128},{192,160},{224,1... | collective-permute-start | bytes 884744 | tf_op jit(solution)/shard_map/ppermute | solution.py:18
  547.5 13.5 %collective-permute-start.21 = (f32[192,384]{0,1:T(8,128)}, f32[192,384]{0,1:T(8,128)}, u32[]{:S(2)}, u32[]{:S(2)}) collective-permute-start(f32[192,384]{0,1:T(8,128)} %get-tuple-element.11), channel_id=1, source_target_pairs={{0,32},{32,64},{64,96},{96,128},{128,160},{160,192},{192,224},{224... | collective-permute-start | bytes 884744 | tf_op jit(solution)/shard_map/ppermute | solution.py:18
  548.5 16.1 %collective-permute-start.22 = (f32[192,384]{0,1:T(8,128)}, f32[192,384]{0,1:T(8,128)}, u32[]{:S(2)}, u32[]{:S(2)}) collective-permute-start(f32[192,384]{0,1:T(8,128)} %get-tuple-element.10), channel_id=1, source_target_pairs={{1,0},{2,1},{3,2},{4,3},{5,4},{6,5},{7,6},{8,7},{9,8},{10,9},{11,1... | collective-permute-start | bytes 884744 | tf_op jit(solution)/shard_map/ppermute | solution.py:24
  549.8 18.9 %collective-permute-start.23 = (f32[192,384]{0,1:T(8,128)S(1)}, f32[192,384]{0,1:T(8,128)}, u32[]{:S(2)}, u32[]{:S(2)}) collective-permute-start(f32[192,384]{0,1:T(8,128)S(1)} %get-tuple-element.9), channel_id=1, source_target_pairs={{0,1},{1,2},{2,3},{3,4},{4,5},{5,6},{6,7},{7,8},{8,9},{9,10},{10,1... | collective-permute-start | bytes 884744 | tf_op jit(solution)/shard_map/ppermute | solution.py:24
